TPU v7x, 1024 devices: a whole 4x4x32 slice. The times are simulated.
1024 devices in a mesh: group: 128 (over z_lo, y, core), dev: 8 (over z_hi, x).
Axes of the slice: x: 4, y: 4, z: 32 (z_hi: 2, z_lo: 16; z = z_hi * 16 + z_lo), core: 2. Of those that a mesh axis runs over, the one named last changes fastest.
Arguments:
- initial_dofs: float32 [56, 9, 32768], P(None, None, ('group', 'dev')), may hold values from -6 to 6
- jacobians: float32 [3, 9, 9, 32768], P(None, None, None, ('group', 'dev')), may hold values from -0.9 to 0.9
- stiffness: float32 [3, 56, 56], replicated, may hold values from -0.75 to 0.75
- projection: float32 [4, 21, 56], replicated, may hold values from -0.75 to 0.75
- minus_root: float32 [4, 9, 9, 32768], P(None, None, None, ('group', 'dev')), may hold values from -1.2 to 1.2
- plus_flux: float32 [4, 9, 9, 32768], P(None, None, None, ('group', 'dev')), may hold values from -0.9 to 0.9
- cluster_id: int32 [32768], P(('group', 'dev')), may hold values from 0 to 2, as said below
- neighbours: int32 [2, 4, 32768], P(None, None, ('group', 'dev')), may hold values from 0 to 159, as said below
- send_faces: int32 [4, 8192], P(None, ('group', 'dev')), may hold values from 0 to 127, as said below
Outputs:
- final_dofs: float32 [56, 9, 32768], P(None, None, ('group', 'dev'))
Inputs may be any that keep to these rules, and one draw needn't show every extreme that they name: `cluster_id`: the 32 consecutive tetrahedra of each partition hold at most 16 of cluster 2, and some partition holds exactly 16. `neighbours`: row 0: for face f of tetrahedron e, either f2 * 32 + e2 naming face f2 of tetrahedron e2 of the same partition (the pairing is symmetric), or 128 + p * 8 + s naming slot s of direction p (0: group index - 1, 1: group index + 1, 2: dev index - 1, 3: dev index + 1); in each partition every slot is named by exactly one face. Row 1: the face number of the adjoining face in its own tetrahedron. `send_faces`: entry (p, s) of a partition is f * 32 + e for its face f of tetrahedron e whose row 0 code is 128 + p * 8 + s; that face adjoins the face at entry (opposite of p, s) of the partition in direction p.
All inputs are finite; a program needn't handle non-finite values.
Results may differ from a plain program's by a relative error of at most 0.0003.
Values sent between devices are 32-bit elements; how exact they have to be, the bound alone decides.
A program may use at most 128 MiB of HBM per device.

v0:
```python
import functools
import math

import jax
import jax.numpy as jnp
from jax import lax
from jax.experimental import pallas as pl
from jax.experimental.pallas import tpu as pltpu
from jax.sharding import PartitionSpec as P

TERMS = 6
STEPS = 4
MESH = pl.DeviceIdType.MESH
f32, bf16 = jnp.float32, jnp.bfloat16

M, Q, E, FM = 56, 9, 32, 24
W = 384
K3 = 176
TR = 216


def weights(power, offset):
    start, end = offset * 0.25, offset * 0.25 + 0.25
    return (end ** (power + 1) - start ** (power + 1)) / math.factorial(power + 1)


def split(x):
    hi = x.astype(bf16)
    return hi, (x - hi.astype(f32)).astype(bf16)


def stacked(x):
    return jnp.concatenate(split(x), axis=0)


def dot3(stack, x):
    rows = stack.shape[0] // 2
    hi, lo = split(x)
    both = jnp.dot(stack, hi, preferred_element_type=f32)
    return both[:rows] + both[rows:] + jnp.dot(stack[:rows], lo, preferred_element_type=f32)


def lane_group(rows):
    return lax.broadcasted_iota(jnp.int32, (rows, 128), 1) // E


def spread(v):
    group = lane_group(v.shape[0])
    odd, high = (group % 2) == 1, group >= 2
    even = jnp.where(odd, pltpu.roll(v, 32, 1), v)
    other = jnp.where(odd, v, pltpu.roll(v, 96, 1))
    even_r, other_r = pltpu.roll(even, 64, 1), pltpu.roll(other, 64, 1)
    return (
        jnp.where(high, even_r, even),
        jnp.where(high, other_r, other),
        jnp.where(high, even, even_r),
        jnp.where(high, other, other_r),
    )


def star_product(x, star):
    parts = [[], [], []]
    for tile in range(M // 8):
        rows = x[tile * 8 : tile * 8 + 8]
        wide = (
            *spread(rows[:, :128]),
            *spread(rows[:, 128:256]),
            spread(rows[:, 256:])[0],
        )
        for d in range(3):
            lanes = []
            for t in range(3):
                cut = slice(t * 128, t * 128 + 128)
                total = wide[0] * star[d * Q, :, cut]
                for i in range(1, Q):
                    total = total + wide[i] * star[d * Q + i, :, cut]
                lanes.append(total)
            parts[d].append(jnp.concatenate(lanes, axis=1))
    pad = [jnp.zeros((K3 - 3 * M, W), f32)]
    return jnp.concatenate(parts[0] + parts[1] + parts[2] + pad, axis=0)


def operator(x, star, s_stack):
    return dot3(s_stack[...], star_product(x, star))[:M]


def to_face_lanes(t):
    group = lane_group(FM)
    out = []
    for q in range(Q):
        tile, g = q // 4, q % 4
        cut = slice(tile * 128, tile * 128 + 128)
        total = None
        for f in range(4):
            piece = t[f * FM : f * FM + FM, cut]
            piece = pltpu.roll(piece, (32 * (f - g)) % 128, 1) if f != g else piece
            total = piece if total is None else jnp.where(group == f, piece, total)
        out.append(total)
    return out


def to_quantity_lanes(flux):
    group = lane_group(FM)
    rows = []
    for f in range(4):
        lanes = []
        for t in range(3):
            total = jnp.zeros((FM, 128), f32)
            for j in range(4 * t, min(4 * t + 4, Q)):
                g = j % 4
                piece = pltpu.roll(flux[j], (32 * (g - f)) % 128, 1) if f != g else flux[j]
                total = jnp.where(group == g, piece, total)
            lanes.append(total)
        rows.append(jnp.concatenate(lanes, axis=1))
    return jnp.concatenate(rows, axis=0)


def contract(rows, table):
    out = []
    for j in range(Q):
        total = None
        for i in range(Q):
            left = rows[i].reshape(FM // 8, 8, 128)
            term = left * table[i * Q + j][None]
            total = term if total is None else total + term
        out.append(total.reshape(FM, 128))
    return out


def kernel(
    axes,
    dofs,
    jac,
    stiff,
    proj,
    root,
    plus_in,
    cluster,
    codes,
    out,
    star,
    minus,
    plus,
    s_stack,
    p_stack,
    pt_stack,
    p_rows,
    coef,
    mask,
    pick,
    owed,
    current,
    base,
    portion,
    pending,
    send_buf,
    recv_buf,
    send_sem,
    recv_sem,
):
    group, dev = lax.axis_index("group"), lax.axis_index("dev")
    n_group, n_dev = axes
    links = (
        (group > 0, {"group": group - 1}, 1),
        (group < n_group - 1, {"group": group + 1}, 0),
        (dev > 0, {"dev": dev - 1}, 3),
        (dev < n_dev - 1, {"dev": dev + 1}, 2),
    )
    send_buf[...] = jnp.zeros_like(send_buf)
    recv_buf[...] = jnp.zeros_like(recv_buf)
    barrier = pltpu.get_barrier_semaphore()
    for there, peer, _ in links:

        @pl.when(there)
        def _():
            pl.semaphore_signal(barrier, inc=1, device_id=peer, device_id_type=MESH)

    kind = cluster[...]
    rate = jnp.where(kind == 2, 4.0, jnp.where(kind == 1, 2.0, 1.0)).astype(f32)
    rate4 = jnp.concatenate([rate] * 4, axis=1)
    kind4 = jnp.concatenate([kind] * 4, axis=1)
    kind12 = jnp.broadcast_to(jnp.concatenate([kind4] * 3, axis=1), (8, W))
    for d in range(3):
        for i in range(Q):
            row = [
                0.5 * rate * (jac[i, j, d : d + 1, :] + jac[j, i, d : d + 1, :]) for j in range(Q)
            ]
            row = jnp.concatenate(row + [jnp.zeros((1, W - Q * E), f32)], axis=1)
            star[d * Q + i] = jnp.broadcast_to(row, (8, W))
    roots = []
    for i in range(Q):
        roots.append(jnp.concatenate([root[i, :, f, :] for f in range(4)], axis=1))
        row = jnp.concatenate([plus_in[i, :, f, :] for f in range(4)], axis=1) * rate4
        for j in range(Q):
            plus[i * Q + j] = jnp.broadcast_to(row[j : j + 1], (8, 128))
    for i in range(Q):
        for j in range(i, Q):
            row = jnp.sum(roots[i] * roots[j], axis=0, keepdims=True) * rate4
            row = jnp.broadcast_to(row, (8, 128))
            minus[i * Q + j] = row
            minus[j * Q + i] = row
    stiff_rows = [stiff[d] - jnp.transpose(stiff[d], (1, 0)) for d in range(3)]
    stiff_rows = jnp.concatenate(stiff_rows + [jnp.zeros((M, K3 - 3 * M), f32)], axis=1)
    s_stack[...] = stacked(jnp.concatenate([stiff_rows, jnp.zeros((8, K3), f32)], axis=0))
    p_rows[...] = jnp.zeros_like(p_rows)
    for f in range(4):
        p_rows[f * FM : f * FM + 21, 0:M] = proj[:, f, :]
    p_stack[...] = stacked(p_rows[...])
    pt_stack[...] = stacked(jnp.transpose(p_rows[...], (1, 0)))
    for u in range(STEPS):
        first = [kind12 == 2, kind12 == 1]
        starting = (True, first[0], first[0] | first[1], first[0])[u]
        mask[u] = jnp.ones((8, W), f32) if u == 0 else jnp.where(starting, 1.0, 0.0).astype(f32)
        for k in range(TERMS):
            coef[u * TERMS + k] = jnp.where(
                first[0],
                weights(k, 0),
                jnp.where(first[1], weights(k, u % 2), weights(k, u)),
            ).astype(f32)
    mask[STEPS] = jnp.ones((8, W), f32)
    code = jnp.concatenate([codes[0, f : f + 1, :] for f in range(4)], axis=1)
    local = lax.broadcasted_iota(jnp.int32, (128, 128), 0) == code
    local = jnp.where(local, 1.0, 0.0).astype(f32).astype(bf16)
    pick[...] = jnp.concatenate([local, local], axis=0)
    remote = lax.broadcasted_iota(jnp.int32, (32, 128), 0) + 128 == code
    remote = jnp.where(remote, 1.0, 0.0).astype(f32).astype(bf16)
    owed[...] = jnp.concatenate([remote, remote], axis=1)
    current[...] = jnp.zeros_like(current)
    current[:, 0 : Q * E] = jnp.transpose(dofs[...].reshape(Q * E, M), (1, 0))
    base[...] = jnp.zeros_like(base)
    pending[...] = jnp.zeros_like(pending)

    def tall(row):
        return jnp.broadcast_to(row[None], (M // 8, 8, W)).reshape(M, W)

    def exchange(u, p):
        there, peer, back = links[p]
        return pltpu.make_async_remote_copy(
            src_ref=send_buf.at[u, p],
            dst_ref=recv_buf.at[u, back],
            send_sem=send_sem.at[u, p],
            recv_sem=recv_sem.at[u, back],
            device_id=peer,
            device_id_type=MESH,
        )

    def landed(u, p):
        there, peer, _ = links[p]
        return pltpu.make_async_remote_copy(
            src_ref=send_buf.at[u, p],
            dst_ref=recv_buf.at[u, p],
            send_sem=send_sem.at[u, p],
            recv_sem=recv_sem.at[u, p],
            device_id=peer,
            device_id_type=MESH,
        )

    def substep(u, first):
        starting = tall(mask[u]) > 0.5
        x = jnp.where(starting, current[...], base[...])
        base[...] = x

        def term(k, carry):
            x, total = carry
            x = operator(x, star, s_stack)
            return x, total + tall(coef[u * TERMS + k]) * x

        x, total = lax.fori_loop(1, TERMS, term, (x, tall(coef[u * TERMS]) * x))
        portion[...] = total
        padded = jnp.concatenate([total, jnp.zeros((8, W), f32)], axis=0)
        traces = to_face_lanes(dot3(p_stack[...], padded))
        both = jnp.concatenate(
            split(jnp.concatenate(traces + [jnp.zeros((8, 128), f32)], axis=0)), axis=1
        )
        outgoing = lax.dot_general(
            owed[...], both, (((1,), (1,)), ((), ())), preferred_element_type=f32
        )
        for p in range(4):
            send_buf[u, p, :, 0:224] = outgoing[p * 8 : p * 8 + 8]
        if first:
            pl.semaphore_wait(barrier, sum(there.astype(jnp.int32) for there, _, _ in links))

        for p in (3, 2, 0, 1):

            @pl.when(links[p][0])
            def _():
                exchange(u, p).start()

        taken = jnp.dot(both, pick[...], preferred_element_type=f32)
        taken = [taken[q * FM : q * FM + FM] for q in range(Q)]
        own = contract(traces, minus)
        flux = [a - b for a, b in zip(contract(taken, plus), own)]
        pending[...] = (
            jnp.where(starting, 0.0, pending[...])
            + operator(portion[...], star, s_stack)
            + dot3(pt_stack[...], to_quantity_lanes(flux))[:M]
        )
        for p in (0, 1, 2, 3):

            @pl.when(links[p][0])
            def _():
                exchange(u, p).wait_send()
                landed(u, p).wait_recv()

        arrived = recv_buf[u].reshape(32, 256)
        arrived = jnp.transpose(arrived, (1, 0))[:224]
        hi, lo = split(arrived)
        spot = owed[:, 0:128]
        taken = jnp.dot(hi, spot, preferred_element_type=f32) + jnp.dot(
            lo, spot, preferred_element_type=f32
        )
        taken = [taken[q * FM : q * FM + FM] for q in range(Q)]
        flux = contract(taken, plus)
        total = pending[...] + dot3(pt_stack[...], to_quantity_lanes(flux))[:M]
        pending[...] = total
        ending = tall(mask[u + 1]) > 0.5
        current[...] = jnp.where(ending, current[...] + total, current[...])

    substep(0, True)

    def later(u, _):
        substep(u, False)
        return 0

    lax.fori_loop(1, STEPS, later, 0)
    out[...] = jnp.transpose(current[:, 0 : Q * E], (1, 0)).reshape(Q, E, M)


def on_device(dofs, jac, stiff, proj, root, plus_in, cluster, codes, send_faces):
    axes = (lax.axis_size("group"), lax.axis_size("dev"))
    scratch = [
        pltpu.VMEM((27, 8, W), f32),
        pltpu.VMEM((81, 8, 128), f32),
        pltpu.VMEM((81, 8, 128), f32),
        pltpu.VMEM((128, K3), bf16),
        pltpu.VMEM((8 * FM, 64), bf16),
        pltpu.VMEM((128, 4 * FM), bf16),
        pltpu.VMEM((4 * FM, 64), f32),
        pltpu.VMEM((STEPS * TERMS, 8, W), f32),
        pltpu.VMEM((STEPS + 1, 8, W), f32),
        pltpu.VMEM((256, 128), bf16),
        pltpu.VMEM((32, 256), bf16),
        pltpu.VMEM((M, W), f32),
        pltpu.VMEM((M, W), f32),
        pltpu.VMEM((M, W), f32),
        pltpu.VMEM((M, W), f32),
        pltpu.VMEM((STEPS, 4, 8, 256), f32),
        pltpu.VMEM((STEPS, 4, 8, 256), f32),
        pltpu.SemaphoreType.DMA((STEPS, 4)),
        pltpu.SemaphoreType.DMA((STEPS, 4)),
    ]
    final = pl.pallas_call(
        functools.partial(kernel, axes),
        out_shape=jax.ShapeDtypeStruct((Q, E, M), f32),
        in_specs=[pl.BlockSpec(memory_space=pltpu.VMEM)] * 8,
        out_specs=pl.BlockSpec(memory_space=pltpu.VMEM),
        scratch_shapes=scratch,
        compiler_params=pltpu.CompilerParams(collective_id=0, has_side_effects=True),
        name="lts_update",
    )(
        jnp.transpose(dofs, (1, 2, 0)),
        jnp.transpose(jac, (1, 2, 0, 3)),
        stiff,
        jnp.transpose(proj, (1, 0, 2)),
        jnp.transpose(root, (1, 2, 0, 3)),
        jnp.transpose(plus_in, (1, 2, 0, 3)),
        cluster.reshape(1, E),
        codes,
    )
    return jnp.transpose(final, (2, 0, 1))


def solution(mesh):
    placed = (
        P(None, None, ("group", "dev")),
        P(None, None, None, ("group", "dev")),
        P(),
        P(),
        P(None, None, None, ("group", "dev")),
        P(None, None, None, ("group", "dev")),
        P(("group", "dev")),
        P(None, None, ("group", "dev")),
        P(None, ("group", "dev")),
    )
    return jax.shard_map(
        on_device,
        mesh=mesh,
        in_specs=placed,
        out_specs=P(None, None, ("group", "dev")),
        check_vma=False,
    )
```

profile of v0, /device:TPU:30, one launch (start us, length us, event | category | flops | bytes accessed | tf_op | source)
XLA Modules:
  0.0 94.3 jit_solution(4741938016745092739)
XLA Ops:
  0.0 92.7 %lts_update.1 = f32[9,32,56]{2,1,0:T(8,128)} custom-call(f32[9,32,56]{2,1,0:T(8,128)} %bitcast.11, f32[9,9,3,32]{3,2,1,0:T(4,128)} %bitcast.8, f32[3,56,56]{2,1,0:T(8,128)} %stiff.1, f32[21,4,56]{2,1,0:T(4,128)} %bitcast.12, f32[9,9,4,32]{3,2,1,0:T(4,128)} %bitcast.9, f32[9,9,4,32]{3,2,1,0:T(4,128)} %bitcast.10, s32[1,32]{1,0:T(1,128)} %bitcast.13, ...), custom_call_target="tpu_custom_call" | custom-call | tf_op jit(solution)/shard_map/lts_update/pallas_call | solution.py:352
  92.7 1.6 %copy.10 = f32[56,9,32]{0,2,1:T(8,128)} copy(f32[56,9,32]{0,2,1:T(8,128)} %bitcast.7) | data formatting | bytes 129024
where the time goes:
time: 94.5 us; the launch traced here: 94.3 us
  Pallas kernels  92.7 us (98%)
  local copies, waits for them, and re-layouts  1.58 us (2%)
    pallas_call x1, Pallas kernels, on_device(): pl.pallas_call(functools.partial(kernel, axes), out_shape=jax.ShapeDtypeS...  92.7 us

commit v1 on v0

--- a/solution.py
+++ b/solution.py
@@ -149,31 +149,43 @@
     mask,
     pick,
     owed,
-    current,
     base,
     portion,
     pending,
+    inbox,
     send_buf,
     recv_buf,
+    fixed_send,
+    fixed_recv,
+    far_star,
+    far_plus,
+    far_place,
+    answer,
     send_sem,
     recv_sem,
+    fixed_sem,
 ):
     group, dev = lax.axis_index("group"), lax.axis_index("dev")
     n_group, n_dev = axes
+    half = n_dev // 2
     links = (
         (group > 0, {"group": group - 1}, 1),
         (group < n_group - 1, {"group": group + 1}, 0),
         (dev > 0, {"dev": dev - 1}, 3),
         (dev < n_dev - 1, {"dev": dev + 1}, 2),
     )
-    send_buf[...] = jnp.zeros_like(send_buf)
-    recv_buf[...] = jnp.zeros_like(recv_buf)
+    far = {2: dev == half, 3: dev == half - 1}
+    is_far = (dev == half) | (dev == half - 1)
+    near = [links[0][0], links[1][0], (dev > 0) & (dev != half)]
+    near.append((dev < n_dev - 1) & (dev != half - 1))
     barrier = pltpu.get_barrier_semaphore()
     for there, peer, _ in links:
 
         @pl.when(there)
         def _():
             pl.semaphore_signal(barrier, inc=1, device_id=peer, device_id_type=MESH)
+
+    send_buf[...] = jnp.zeros_like(send_buf)
 
     kind = cluster[...]
     rate = jnp.where(kind == 2, 4.0, jnp.where(kind == 1, 2.0, 1.0)).astype(f32)
@@ -217,7 +229,6 @@
                 weights(k, 0),
                 jnp.where(first[1], weights(k, u % 2), weights(k, u)),
             ).astype(f32)
-    mask[STEPS] = jnp.ones((8, W), f32)
     code = jnp.concatenate([codes[0, f : f + 1, :] for f in range(4)], axis=1)
     local = lax.broadcasted_iota(jnp.int32, (128, 128), 0) == code
     local = jnp.where(local, 1.0, 0.0).astype(f32).astype(bf16)
@@ -225,105 +236,254 @@
     remote = lax.broadcasted_iota(jnp.int32, (32, 128), 0) + 128 == code
     remote = jnp.where(remote, 1.0, 0.0).astype(f32).astype(bf16)
     owed[...] = jnp.concatenate([remote, remote], axis=1)
-    current[...] = jnp.zeros_like(current)
-    current[:, 0 : Q * E] = jnp.transpose(dofs[...].reshape(Q * E, M), (1, 0))
     base[...] = jnp.zeros_like(base)
+    base[:, 0 : Q * E] = jnp.transpose(dofs[...].reshape(Q * E, M), (1, 0))
     pending[...] = jnp.zeros_like(pending)
 
     def tall(row):
         return jnp.broadcast_to(row[None], (M // 8, 8, W)).reshape(M, W)
 
-    def exchange(u, p):
-        there, peer, back = links[p]
+    def exchange(u, p, slot):
         return pltpu.make_async_remote_copy(
             src_ref=send_buf.at[u, p],
-            dst_ref=recv_buf.at[u, back],
+            dst_ref=recv_buf.at[u, slot],
             send_sem=send_sem.at[u, p],
-            recv_sem=recv_sem.at[u, back],
-            device_id=peer,
+            recv_sem=recv_sem.at[u, slot],
+            device_id=links[p][1],
             device_id_type=MESH,
         )
 
-    def landed(u, p):
-        there, peer, _ = links[p]
+    def send(u, p):
+        exchange(u, p, links[p][2]).start()
+
+    def collect(u, p):
+        exchange(u, p, links[p][2]).wait_send()
+        exchange(u, p, p).wait_recv()
+
+    def fixed(p):
         return pltpu.make_async_remote_copy(
-            src_ref=send_buf.at[u, p],
-            dst_ref=recv_buf.at[u, p],
-            send_sem=send_sem.at[u, p],
-            recv_sem=recv_sem.at[u, p],
-            device_id=peer,
+            src_ref=fixed_send,
+            dst_ref=fixed_recv,
+            send_sem=fixed_sem.at[0],
+            recv_sem=fixed_sem.at[1],
+            device_id=links[p][1],
             device_id_type=MESH,
         )
 
-    def substep(u, first):
-        starting = tall(mask[u]) > 0.5
-        x = jnp.where(starting, current[...], base[...])
-        base[...] = x
-
+    def expand(u, x, table):
         def term(k, carry):
             x, total = carry
-            x = operator(x, star, s_stack)
+            x = operator(x, table, s_stack)
             return x, total + tall(coef[u * TERMS + k]) * x
 
-        x, total = lax.fori_loop(1, TERMS, term, (x, tall(coef[u * TERMS]) * x))
-        portion[...] = total
+        return lax.fori_loop(1, TERMS, term, (x, tall(coef[u * TERMS]) * x))[1]
+
+    def project(total):
         padded = jnp.concatenate([total, jnp.zeros((8, W), f32)], axis=0)
         traces = to_face_lanes(dot3(p_stack[...], padded))
-        both = jnp.concatenate(
-            split(jnp.concatenate(traces + [jnp.zeros((8, 128), f32)], axis=0)), axis=1
+        rows = jnp.concatenate(traces + [jnp.zeros((8, 128), f32)], axis=0)
+        return traces, jnp.concatenate(split(rows), axis=1)
+
+    def rows_for(places, both):
+        return lax.dot_general(
+            places, both, (((1,), (1,)), ((), ())), preferred_element_type=f32
         )
-        outgoing = lax.dot_general(
-            owed[...], both, (((1,), (1,)), ((), ())), preferred_element_type=f32
+
+    def lifted(flux):
+        return dot3(pt_stack[...], to_quantity_lanes(flux))[:M]
+
+    def placed(rows, places, count):
+        hi, lo = split(jnp.transpose(rows, (1, 0))[:count])
+        return jnp.dot(hi, places, preferred_element_type=f32) + jnp.dot(
+            lo, places, preferred_element_type=f32
         )
+
+    def received(rows, places, table):
+        taken = placed(rows, places, 224)
+        return lifted(contract([taken[q * FM : q * FM + FM] for q in range(Q)], table))
+
+    def absorb():
+        pending[...] += received(inbox[...], owed[:, 0:128], plus)
+
+    def stay(u, traces, both):
+        taken = jnp.dot(both, pick[...], preferred_element_type=f32)
+        taken = [taken[q * FM : q * FM + FM] for q in range(Q)]
+        flux = [a - b for a, b in zip(contract(taken, plus), contract(traces, minus))]
+        pending[...] = (
+            jnp.where(tall(mask[u]) > 0.5, 0.0, pending[...])
+            + operator(portion[...], star, s_stack)
+            + lifted(flux)
+        )
+
+    def pack_fixed():
+        for p, there in far.items():
+
+            @pl.when(there)
+            def _():
+                v = owed[:, 0:128].astype(f32)[p * 8 : p * 8 + 8]
+                v = v + pltpu.roll(v, 64, 1)
+                v = v + pltpu.roll(v, 32, 1)
+                v = jnp.concatenate([v] * 3, axis=1)
+                lane = lax.broadcasted_iota(jnp.int32, (8, W), 1) // E
+                chosen = [jnp.where(lane == j, v, 0.0) for j in range(Q)]
+                chosen = jnp.concatenate(chosen + [jnp.zeros((56, W), f32)], axis=0).astype(bf16)
+                rows = jnp.concatenate([star[:, 0, :], jnp.zeros((5, W), f32)], axis=0)
+                hi, lo = split(rows)
+                fixed_send[0:32] = rows_for(hi, chosen) + rows_for(lo, chosen)
+                lane = lax.broadcasted_iota(jnp.int32, (1, 128), 1)
+                fast = jnp.where(kind4 == 2, 1.0, 0.0).astype(f32)
+                rows = jnp.concatenate(
+                    [
+                        plus[:, 0, :] * fast,
+                        (lane % E).astype(f32),
+                        (lane // E).astype(f32),
+                        jnp.zeros((45, 128), f32),
+                    ],
+                    axis=0,
+                )
+                rows = rows_for(owed[...], jnp.concatenate(split(rows), axis=1))
+                fixed_send[32:40] = rows[p * 8 : p * 8 + 8]
+
+    def unpack_fixed():
+        for p, there in far.items():
+
+            @pl.when(there)
+            def _():
+                fixed(p).wait_send()
+                fixed(p).wait_recv()
+                row = lax.broadcasted_iota(jnp.int32, (128, W), 0)
+                lane = lax.broadcasted_iota(jnp.int32, (128, W), 1)
+                wide = (lane // E == row // 8) & (lane % E == p * 8 + row % 8)
+                wide = jnp.where(wide, 1.0, 0.0).astype(f32).astype(bf16)
+                hi, lo = split(fixed_recv[0:32])
+                rows = jnp.dot(hi, wide, preferred_element_type=f32)
+                rows = rows + jnp.dot(lo, wide, preferred_element_type=f32)
+                for r in range(27):
+                    far_star[r] = jnp.broadcast_to(rows[r : r + 1], (8, W))
+                rows = fixed_recv[32:40]
+                lane = lax.broadcasted_iota(jnp.int32, (8, 128), 1).astype(f32)
+                element, face = rows[:, 81:82], rows[:, 82:83]
+                owner = jnp.where(lane == element, 1.0, 0.0).astype(f32).astype(bf16)
+                same = rows_for(owner, owner)
+                order = lax.broadcasted_iota(jnp.int32, (8, 8), 1).astype(f32)
+                leader = jnp.min(jnp.where(same > 0.5, order, 8.0), axis=1, keepdims=True)
+                spot = jnp.where(lane == face * E + (p * 8) + leader, 1.0, 0.0).astype(f32)
+                blank = [jnp.zeros((8, 128), f32)]
+                spots = jnp.concatenate(blank * p + [spot] + blank * (3 - p), axis=0).astype(bf16)
+                far_place[...] = jnp.concatenate([spots, spots], axis=1)
+                rows = jnp.concatenate(blank * p + [rows] + blank * (3 - p), axis=0)
+                rows = placed(rows, spots, 88)
+                for r in range(81):
+                    far_plus[r] = jnp.broadcast_to(rows[r : r + 1], (8, 128))
+
+    def pair(h, _):
+        u, v = 2 * h, 2 * h + 1
+        total = expand(u, base[...], star)
+        portion[...] = total
+        traces, both = project(total)
+        outgoing = rows_for(owed[...], both)
         for p in range(4):
             send_buf[u, p, :, 0:224] = outgoing[p * 8 : p * 8 + 8]
-        if first:
+
+        @pl.when(h == 0)
+        def _():
+            pack_fixed()
             pl.semaphore_wait(barrier, sum(there.astype(jnp.int32) for there, _, _ in links))
 
         for p in (3, 2, 0, 1):
 
             @pl.when(links[p][0])
             def _():
-                exchange(u, p).start()
-
-        taken = jnp.dot(both, pick[...], preferred_element_type=f32)
-        taken = [taken[q * FM : q * FM + FM] for q in range(Q)]
-        own = contract(traces, minus)
-        flux = [a - b for a, b in zip(contract(taken, plus), own)]
-        pending[...] = (
-            jnp.where(starting, 0.0, pending[...])
-            + operator(portion[...], star, s_stack)
-            + dot3(pt_stack[...], to_quantity_lanes(flux))[:M]
-        )
-        for p in (0, 1, 2, 3):
-
-            @pl.when(links[p][0])
-            def _():
-                exchange(u, p).wait_send()
-                landed(u, p).wait_recv()
-
-        arrived = recv_buf[u].reshape(32, 256)
-        arrived = jnp.transpose(arrived, (1, 0))[:224]
-        hi, lo = split(arrived)
-        spot = owed[:, 0:128]
-        taken = jnp.dot(hi, spot, preferred_element_type=f32) + jnp.dot(
-            lo, spot, preferred_element_type=f32
-        )
-        taken = [taken[q * FM : q * FM + FM] for q in range(Q)]
-        flux = contract(taken, plus)
-        total = pending[...] + dot3(pt_stack[...], to_quantity_lanes(flux))[:M]
-        pending[...] = total
-        ending = tall(mask[u + 1]) > 0.5
-        current[...] = jnp.where(ending, current[...] + total, current[...])
-
-    substep(0, True)
-
-    def later(u, _):
-        substep(u, False)
+                send(u, p)
+
+        for p, there in far.items():
+
+            @pl.when(there & (h == 0))
+            def _():
+                fixed(p).start()
+
+        stay(u, traces, both)
+        inbox[...] = jnp.zeros_like(inbox)
+        for p in range(4):
+
+            @pl.when(near[p])
+            def _():
+                collect(u, p)
+                inbox[p * 8 : p * 8 + 8] = recv_buf[u, p]
+
+        absorb()
+
+        @pl.when(is_far)
+        def _():
+            x = jnp.where(tall(mask[v]) > 0.5, base[...] + pending[...], base[...])
+            early = rows_for(owed[...], project(expand(v, x, star))[1])
+            for p, there in far.items():
+
+                @pl.when(there)
+                def _():
+                    send_buf[v, p, :, 0:224] = early[p * 8 : p * 8 + 8]
+                    send(v, p)
+
+            inbox[...] = jnp.zeros_like(inbox)
+            for p, there in far.items():
+
+                @pl.when(there)
+                def _():
+                    collect(u, p)
+                    inbox[p * 8 : p * 8 + 8] = recv_buf[u, p]
+
+            absorb()
+
+        x = jnp.where(tall(mask[v]) > 0.5, base[...] + pending[...], base[...])
+        base[...] = x
+        total = expand(v, x, star)
+        portion[...] = total
+        traces, both = project(total)
+        outgoing = rows_for(owed[...], both)
+        for p in range(4):
+
+            @pl.when(near[p])
+            def _():
+                send_buf[v, p, :, 0:224] = outgoing[p * 8 : p * 8 + 8]
+                send(v, p)
+
+        stay(v, traces, both)
+        inbox[...] = jnp.zeros_like(inbox)
+
+        @pl.when(is_far)
+        def _():
+            @pl.when(h == 0)
+            def _():
+                unpack_fixed()
+
+            mine = send_buf[u].reshape(32, 256)
+            x = received(mine, far_place[:, 0:128], far_plus)
+            both = project(expand(0, x, far_star))[1]
+            answer[:, 0:224] = rows_for(far_place[...], both)
+            for p, there in far.items():
+
+                @pl.when(there)
+                def _():
+                    collect(v, p)
+                    rows = slice(p * 8, p * 8 + 8)
+                    inbox[rows, 0:224] = recv_buf[v, p, :, 0:224] + answer[rows, 0:224]
+
+        for p in range(4):
+
+            @pl.when(near[p])
+            def _():
+                collect(v, p)
+                inbox[p * 8 : p * 8 + 8] = recv_buf[v, p]
+
+        absorb()
+        last = h == STEPS // 2 - 1
+        following = jnp.minimum(v + 1, STEPS - 1)
+        ending = (tall(mask[following]) > 0.5) | last
+        base[...] = jnp.where(ending, base[...] + pending[...], base[...])
         return 0
 
-    lax.fori_loop(1, STEPS, later, 0)
-    out[...] = jnp.transpose(current[:, 0 : Q * E], (1, 0)).reshape(Q, E, M)
+    lax.fori_loop(0, STEPS // 2, pair, 0)
+    out[...] = jnp.transpose(base[:, 0 : Q * E], (1, 0)).reshape(Q, E, M)
 
 
 def on_device(dofs, jac, stiff, proj, root, plus_in, cluster, codes, send_faces):
@@ -337,17 +497,24 @@
         pltpu.VMEM((128, 4 * FM), bf16),
         pltpu.VMEM((4 * FM, 64), f32),
         pltpu.VMEM((STEPS * TERMS, 8, W), f32),
-        pltpu.VMEM((STEPS + 1, 8, W), f32),
+        pltpu.VMEM((STEPS, 8, W), f32),
         pltpu.VMEM((256, 128), bf16),
         pltpu.VMEM((32, 256), bf16),
         pltpu.VMEM((M, W), f32),
         pltpu.VMEM((M, W), f32),
         pltpu.VMEM((M, W), f32),
-        pltpu.VMEM((M, W), f32),
+        pltpu.VMEM((32, 256), f32),
         pltpu.VMEM((STEPS, 4, 8, 256), f32),
         pltpu.VMEM((STEPS, 4, 8, 256), f32),
+        pltpu.VMEM((40, 128), f32),
+        pltpu.VMEM((40, 128), f32),
+        pltpu.VMEM((27, 8, W), f32),
+        pltpu.VMEM((81, 8, 128), f32),
+        pltpu.VMEM((32, 256), bf16),
+        pltpu.VMEM((32, 256), f32),
         pltpu.SemaphoreType.DMA((STEPS, 4)),
         pltpu.SemaphoreType.DMA((STEPS, 4)),
+        pltpu.SemaphoreType.DMA((2,)),
     ]
     final = pl.pallas_call(
         functools.partial(kernel, axes),

time: 94.5 us -> 78.1 us (0.83)
  the two profiles are of different devices: /device:TPU:30 before, /device:TPU:22 now
where the time goes in v1:
time: 78.1 us; the launch traced here: 77.9 us
  Pallas kernels  76.3 us (98%)
  local copies, waits for them, and re-layouts  1.58 us (2%)
    pallas_call x1, Pallas kernels, on_device(): pl.pallas_call(functools.partial(kernel, axes), out_shape=jax.ShapeDtypeS...  76.3 us
    unnamed x1, local copies, waits for them, and re-layouts  1.58 us

profile of v1, /device:TPU:22, one launch (start us, length us, event | category | flops | bytes accessed | tf_op | source)
XLA Modules:
  0.0 77.9 jit_solution(1693233722633766701)
XLA Ops:
  0.0 76.3 %lts_update.1 = f32[9,32,56]{2,1,0:T(8,128)} custom-call(f32[9,32,56]{2,1,0:T(8,128)} %bitcast.11, f32[9,9,3,32]{3,2,1,0:T(4,128)} %bitcast.8, f32[3,56,56]{2,1,0:T(8,128)} %stiff.1, f32[21,4,56]{2,1,0:T(4,128)} %bitcast.12, f32[9,9,4,32]{3,2,1,0:T(4,128)} %bitcast.9, f32[9,9,4,32]{3,2,1,0:T(4,128)} %bitcast.10, s32[1,32]{1,0:T(1,128)} %bitcast.13, ...), custom_call_target="tpu_custom_call" | custom-call | tf_op jit(solution)/shard_map/lts_update/pallas_call | solution.py:519
  76.3 1.6 %copy.10 = f32[56,9,32]{0,2,1:T(8,128)} copy(f32[56,9,32]{0,2,1:T(8,128)} %bitcast.7) | data formatting | bytes 129024

commit v2 on v1

--- a/solution.py
+++ b/solution.py
@@ -58,30 +58,36 @@
     )
 
 
-def star_product(x, star):
-    parts = [[], [], []]
-    for tile in range(M // 8):
+def quad(stack, y):
+    rows = stack.shape[0] // 2
+    both = jnp.dot(stack, jnp.concatenate(split(y), axis=1), preferred_element_type=f32)
+    return (both[:rows, :128] + both[rows:, :128]) + (both[:rows, 128:] + both[rows:, 128:])
+
+
+def operator(x, star, s_stack):
+    tiles = M // 8
+    wide = []
+    for tile in range(tiles):
         rows = x[tile * 8 : tile * 8 + 8]
-        wide = (
-            *spread(rows[:, :128]),
-            *spread(rows[:, 128:256]),
-            spread(rows[:, 256:])[0],
+        wide.append(
+            (*spread(rows[:, :128]), *spread(rows[:, 128:256]), spread(rows[:, 256:])[0])
         )
-        for d in range(3):
-            lanes = []
-            for t in range(3):
-                cut = slice(t * 128, t * 128 + 128)
-                total = wide[0] * star[d * Q, :, cut]
-                for i in range(1, Q):
-                    total = total + wide[i] * star[d * Q + i, :, cut]
-                lanes.append(total)
-            parts[d].append(jnp.concatenate(lanes, axis=1))
-    pad = [jnp.zeros((K3 - 3 * M, W), f32)]
-    return jnp.concatenate(parts[0] + parts[1] + parts[2] + pad, axis=0)
-
-
-def operator(x, star, s_stack):
-    return dot3(s_stack[...], star_product(x, star))[:M]
+
+    def weighted(tile, at):
+        total = wide[tile][0] * star[at]
+        for i in range(1, Q):
+            total = total + wide[tile][i] * star[i * 7 + at]
+        return total
+
+    blank = [jnp.zeros((8, 128), f32)]
+    last = [weighted(tile, 6) for tile in range(tiles)]
+    rolled = [pltpu.roll(y, 96, 1) for y in last] + [pltpu.roll(y, 64, 1) for y in last]
+    stack = s_stack[...]
+    out = [quad(stack, jnp.concatenate(last + rolled + blank, axis=0))]
+    for t in range(2):
+        y = [weighted(tile, d * 2 + t) for d in range(3) for tile in range(tiles)]
+        out.append(quad(stack, jnp.concatenate(y + blank, axis=0)))
+    return jnp.concatenate([out[1][:M], out[2][:M], out[0][:M]], axis=1)
 
 
 def to_face_lanes(t):
@@ -129,6 +135,17 @@
 
 def kernel(
     axes,
+    *refs,
+):
+    inputs, (out, *refs) = refs[:8], refs[8:]
+    held, copy_sem, refs = refs[:8], refs[8], refs[9:]
+    copies = [pltpu.make_async_copy(a, b, copy_sem.at[i]) for i, (a, b) in enumerate(zip(inputs, held))]
+    body(axes, copies, *held, out, *refs)
+
+
+def body(
+    axes,
+    copies,
     dofs,
     jac,
     stiff,
@@ -185,20 +202,32 @@
         def _():
             pl.semaphore_signal(barrier, inc=1, device_id=peer, device_id_type=MESH)
 
+    for copy in copies:
+        copy.start()
     send_buf[...] = jnp.zeros_like(send_buf)
+    fixed_send[...] = jnp.zeros_like(fixed_send)
+
+    for copy in copies:
+        copy.wait()
 
     kind = cluster[...]
     rate = jnp.where(kind == 2, 4.0, jnp.where(kind == 1, 2.0, 1.0)).astype(f32)
     rate4 = jnp.concatenate([rate] * 4, axis=1)
     kind4 = jnp.concatenate([kind] * 4, axis=1)
     kind12 = jnp.broadcast_to(jnp.concatenate([kind4] * 3, axis=1), (8, W))
+    last = [[] for _ in range(Q)]
     for d in range(3):
         for i in range(Q):
             row = [
                 0.5 * rate * (jac[i, j, d : d + 1, :] + jac[j, i, d : d + 1, :]) for j in range(Q)
             ]
-            row = jnp.concatenate(row + [jnp.zeros((1, W - Q * E), f32)], axis=1)
-            star[d * Q + i] = jnp.broadcast_to(row, (8, W))
+            last[i].append(row[8])
+            for t in range(2):
+                tile = jnp.concatenate(row[4 * t : 4 * t + 4], axis=1)
+                star[i * 7 + d * 2 + t] = jnp.broadcast_to(tile, (8, 128))
+    for i in range(Q):
+        tile = jnp.concatenate(last[i] + [jnp.zeros((1, E), f32)], axis=1)
+        star[i * 7 + 6] = jnp.broadcast_to(tile, (8, 128))
     roots = []
     for i in range(Q):
         roots.append(jnp.concatenate([root[i, :, f, :] for f in range(4)], axis=1))
@@ -323,13 +352,14 @@
                 v = owed[:, 0:128].astype(f32)[p * 8 : p * 8 + 8]
                 v = v + pltpu.roll(v, 64, 1)
                 v = v + pltpu.roll(v, 32, 1)
-                v = jnp.concatenate([v] * 3, axis=1)
-                lane = lax.broadcasted_iota(jnp.int32, (8, W), 1) // E
-                chosen = [jnp.where(lane == j, v, 0.0) for j in range(Q)]
-                chosen = jnp.concatenate(chosen + [jnp.zeros((56, W), f32)], axis=0).astype(bf16)
-                rows = jnp.concatenate([star[:, 0, :], jnp.zeros((5, W), f32)], axis=0)
+                lane = lax.broadcasted_iota(jnp.int32, (8, 128), 1) // E
+                chosen = [jnp.where(lane == g, v, 0.0) for g in range(4)]
+                chosen = jnp.concatenate(chosen, axis=0).astype(bf16)
+                rows = jnp.concatenate([star[:, 0, :], jnp.zeros((1, 128), f32)], axis=0)
                 hi, lo = split(rows)
-                fixed_send[0:32] = rows_for(hi, chosen) + rows_for(lo, chosen)
+                rows = rows_for(chosen, hi) + rows_for(chosen, lo)
+                rows = jnp.concatenate([rows, jnp.zeros((32, 64), f32)], axis=1)
+                fixed_send[0:16] = rows[:16] + pltpu.roll(rows[16:], 64, 1)
                 lane = lax.broadcasted_iota(jnp.int32, (1, 128), 1)
                 fast = jnp.where(kind4 == 2, 1.0, 0.0).astype(f32)
                 rows = jnp.concatenate(
@@ -342,7 +372,7 @@
                     axis=0,
                 )
                 rows = rows_for(owed[...], jnp.concatenate(split(rows), axis=1))
-                fixed_send[32:40] = rows[p * 8 : p * 8 + 8]
+                fixed_send[16:24] = rows[p * 8 : p * 8 + 8]
 
     def unpack_fixed():
         for p, there in far.items():
@@ -351,16 +381,16 @@
             def _():
                 fixed(p).wait_send()
                 fixed(p).wait_recv()
-                row = lax.broadcasted_iota(jnp.int32, (128, W), 0)
-                lane = lax.broadcasted_iota(jnp.int32, (128, W), 1)
+                row = lax.broadcasted_iota(jnp.int32, (32, 128), 0)
+                lane = lax.broadcasted_iota(jnp.int32, (32, 128), 1)
                 wide = (lane // E == row // 8) & (lane % E == p * 8 + row % 8)
                 wide = jnp.where(wide, 1.0, 0.0).astype(f32).astype(bf16)
-                hi, lo = split(fixed_recv[0:32])
-                rows = jnp.dot(hi, wide, preferred_element_type=f32)
-                rows = rows + jnp.dot(lo, wide, preferred_element_type=f32)
-                for r in range(27):
-                    far_star[r] = jnp.broadcast_to(rows[r : r + 1], (8, W))
-                rows = fixed_recv[32:40]
+                rows = fixed_recv[0:16]
+                rows = jnp.concatenate([rows, pltpu.roll(rows, 64, 1)], axis=0)
+                rows = placed(rows, wide, 64)
+                for r in range(63):
+                    far_star[r] = jnp.broadcast_to(rows[r : r + 1], (8, 128))
+                rows = fixed_recv[16:24]
                 lane = lax.broadcasted_iota(jnp.int32, (8, 128), 1).astype(f32)
                 element, face = rows[:, 81:82], rows[:, 82:83]
                 owner = jnp.where(lane == element, 1.0, 0.0).astype(f32).astype(bf16)
@@ -376,6 +406,12 @@
                 for r in range(81):
                     far_plus[r] = jnp.broadcast_to(rows[r : r + 1], (8, 128))
 
+    def respond(u):
+        mine = send_buf[u].reshape(32, 256)
+        x = received(mine, far_place[:, 0:128], far_plus)
+        both = project(expand(0, x, far_star))[1]
+        answer[:, 0:224] = rows_for(far_place[...], both)
+
     def pair(h, _):
         u, v = 2 * h, 2 * h + 1
         total = expand(u, base[...], star)
@@ -424,6 +460,10 @@
                     send_buf[v, p, :, 0:224] = early[p * 8 : p * 8 + 8]
                     send(v, p)
 
+            @pl.when(h > 0)
+            def _():
+                respond(u)
+
             inbox[...] = jnp.zeros_like(inbox)
             for p, there in far.items():
 
@@ -455,11 +495,8 @@
             @pl.when(h == 0)
             def _():
                 unpack_fixed()
-
-            mine = send_buf[u].reshape(32, 256)
-            x = received(mine, far_place[:, 0:128], far_plus)
-            both = project(expand(0, x, far_star))[1]
-            answer[:, 0:224] = rows_for(far_place[...], both)
+                respond(u)
+
             for p, there in far.items():
 
                 @pl.when(there)
@@ -489,7 +526,16 @@
 def on_device(dofs, jac, stiff, proj, root, plus_in, cluster, codes, send_faces):
     axes = (lax.axis_size("group"), lax.axis_size("dev"))
     scratch = [
-        pltpu.VMEM((27, 8, W), f32),
+        pltpu.VMEM((Q, E, M), f32),
+        pltpu.VMEM((Q, Q, 3, E), f32),
+        pltpu.VMEM((3, M, M), f32),
+        pltpu.VMEM((21, 4, M), f32),
+        pltpu.VMEM((Q, Q, 4, E), f32),
+        pltpu.VMEM((Q, Q, 4, E), f32),
+        pltpu.VMEM((1, E), jnp.int32),
+        pltpu.VMEM((2, 4, E), jnp.int32),
+        pltpu.SemaphoreType.DMA((8,)),
+        pltpu.VMEM((63, 8, 128), f32),
         pltpu.VMEM((81, 8, 128), f32),
         pltpu.VMEM((81, 8, 128), f32),
         pltpu.VMEM((128, K3), bf16),
@@ -506,9 +552,9 @@
         pltpu.VMEM((32, 256), f32),
         pltpu.VMEM((STEPS, 4, 8, 256), f32),
         pltpu.VMEM((STEPS, 4, 8, 256), f32),
-        pltpu.VMEM((40, 128), f32),
-        pltpu.VMEM((40, 128), f32),
-        pltpu.VMEM((27, 8, W), f32),
+        pltpu.VMEM((24, 128), f32),
+        pltpu.VMEM((24, 128), f32),
+        pltpu.VMEM((63, 8, 128), f32),
         pltpu.VMEM((81, 8, 128), f32),
         pltpu.VMEM((32, 256), bf16),
         pltpu.VMEM((32, 256), f32),
@@ -519,7 +565,7 @@
     final = pl.pallas_call(
         functools.partial(kernel, axes),
         out_shape=jax.ShapeDtypeStruct((Q, E, M), f32),
-        in_specs=[pl.BlockSpec(memory_space=pltpu.VMEM)] * 8,
+        in_specs=[pl.BlockSpec(memory_space=pl.ANY)] * 8,
         out_specs=pl.BlockSpec(memory_space=pltpu.VMEM),
         scratch_shapes=scratch,
         compiler_params=pltpu.CompilerParams(collective_id=0, has_side_effects=True),

time: 78.1 us -> 75.2 us (0.963)
  the two profiles are of different devices: /device:TPU:22 before, /device:TPU:15 now
where the time goes in v2:
time: 75.2 us; the launch traced here: 75 us
  Pallas kernels  73.5 us (98%)
  local copies, waits for them, and re-layouts  1.58 us (2%)
    pallas_call x1, Pallas kernels, on_device(): pl.pallas_call(functools.partial(kernel, axes), out_shape=jax.ShapeDtypeS...  73.5 us
    unnamed x1, local copies, waits for them, and re-layouts  1.58 us

profile of v2, /device:TPU:15, one launch (start us, length us, event | category | flops | bytes accessed | tf_op | source)
XLA Modules:
  0.0 75.0 jit_solution(1934919190105179504)
XLA Ops:
  0.0 73.5 %lts_update.1 = f32[9,32,56]{2,1,0:T(8,128)} custom-call(f32[9,32,56]{2,1,0:T(8,128)} %bitcast.11, f32[9,9,3,32]{3,2,1,0:T(4,128)} %bitcast.8, f32[3,56,56]{2,1,0:T(8,128)} %refs_2_.1, f32[21,4,56]{2,1,0:T(4,128)} %bitcast.12, f32[9,9,4,32]{3,2,1,0:T(4,128)} %bitcast.9, f32[9,9,4,32]{3,2,1,0:T(4,128)} %bitcast.10, s32[1,32]{1,0:T(1,128)} %bitcast.13, ...), custom_call_target="tpu_custom_call" | custom-call | tf_op jit(solution)/shard_map/lts_update/pallas_call | solution.py:565
  73.5 1.6 %copy.10 = f32[56,9,32]{0,2,1:T(8,128)} copy(f32[56,9,32]{0,2,1:T(8,128)} %bitcast.7) | data formatting | bytes 129024

commit v3 on v2

--- a/solution.py
+++ b/solution.py
@@ -181,6 +181,10 @@
     send_sem,
     recv_sem,
     fixed_sem,
+    relay_rows,
+    relay_fixed,
+    relay_sem,
+    onward_sem,
 ):
     group, dev = lax.axis_index("group"), lax.axis_index("dev")
     n_group, n_dev = axes
@@ -195,12 +199,25 @@
     is_far = (dev == half) | (dev == half - 1)
     near = [links[0][0], links[1][0], (dev > 0) & (dev != half)]
     near.append((dev < n_dev - 1) & (dev != half - 1))
+    middle = n_group // 2
+    giver = (dev == half - 1) & (group < middle)
+    taker = (dev == half) & (group < middle)
+    relay = (dev == half - 2) & (group >= middle)
     barrier = pltpu.get_barrier_semaphore()
-    for there, peer, _ in links:
-
+
+    def greet(there, peer):
         @pl.when(there)
         def _():
             pl.semaphore_signal(barrier, inc=1, device_id=peer, device_id_type=MESH)
+
+    for p, (there, peer, _) in enumerate(links):
+        greet(there & jnp.logical_not(taker) if p == 2 else there, peer)
+    above = {"group": group + middle, "dev": half - 2}
+    greet(giver | taker, above)
+    greet(relay, {"group": group - middle, "dev": half - 1})
+    greet(relay, {"group": group - middle, "dev": half})
+    callers = sum(there.astype(jnp.int32) for there, _, _ in links)
+    callers = callers + taker.astype(jnp.int32) + 2 * relay.astype(jnp.int32)
 
     for copy in copies:
         copy.start()
@@ -299,6 +316,26 @@
             device_id_type=MESH,
         )
 
+    def hand_over(part):
+        return pltpu.make_async_remote_copy(
+            src_ref=(send_buf.at[0, 3], fixed_send, send_buf.at[1, 3])[part],
+            dst_ref=(relay_rows.at[0], relay_fixed, relay_rows.at[1])[part],
+            send_sem=(send_sem.at[0, 3], fixed_sem.at[0], send_sem.at[1, 3])[part],
+            recv_sem=relay_sem.at[part],
+            device_id=above,
+            device_id_type=MESH,
+        )
+
+    def hand_on(part):
+        return pltpu.make_async_remote_copy(
+            src_ref=(relay_rows.at[0], relay_fixed, relay_rows.at[1])[part],
+            dst_ref=(recv_buf.at[0, 2], fixed_recv, recv_buf.at[1, 2])[part],
+            send_sem=onward_sem.at[part],
+            recv_sem=(recv_sem.at[0, 2], fixed_sem.at[1], recv_sem.at[1, 2])[part],
+            device_id={"group": group - middle, "dev": half},
+            device_id_type=MESH,
+        )
+
     def expand(u, x, table):
         def term(k, carry):
             x, total = carry
@@ -423,22 +460,48 @@
 
         @pl.when(h == 0)
         def _():
+            pl.semaphore_wait(barrier, callers)
+
+        by_relay = giver & (h == 0)
+
+        @pl.when(by_relay)
+        def _():
+            hand_over(0).start()
+
+        for p in (3, 2, 0, 1):
+            there = links[p][0]
+
+            @pl.when(there & jnp.logical_not(by_relay) if p == 3 else there)
+            def _():
+                send(u, p)
+
+        @pl.when(h == 0)
+        def _():
             pack_fixed()
-            pl.semaphore_wait(barrier, sum(there.astype(jnp.int32) for there, _, _ in links))
-
-        for p in (3, 2, 0, 1):
-
-            @pl.when(links[p][0])
-            def _():
-                send(u, p)
+
+        @pl.when(by_relay)
+        def _():
+            hand_over(1).start()
 
         for p, there in far.items():
 
-            @pl.when(there & (h == 0))
+            @pl.when(there & (h == 0) & jnp.logical_not(giver))
             def _():
                 fixed(p).start()
 
+        @pl.when(relay & (h == 0))
+        def _():
+            for part in range(2):
+                hand_over(part).wait_recv()
+                hand_on(part).start()
+
         stay(u, traces, both)
+
+        @pl.when(relay & (h == 0))
+        def _():
+            hand_over(2).wait_recv()
+            hand_on(2).start()
+
         inbox[...] = jnp.zeros_like(inbox)
         for p in range(4):
 
@@ -458,7 +521,14 @@
                 @pl.when(there)
                 def _():
                     send_buf[v, p, :, 0:224] = early[p * 8 : p * 8 + 8]
+
+                @pl.when(there & jnp.logical_not(by_relay) if p == 3 else there)
+                def _():
                     send(v, p)
+
+            @pl.when(by_relay)
+            def _():
+                hand_over(2).start()
 
             @pl.when(h > 0)
             def _():
@@ -520,6 +590,12 @@
         return 0
 
     lax.fori_loop(0, STEPS // 2, pair, 0)
+
+    @pl.when(relay)
+    def _():
+        for part in range(3):
+            hand_on(part).wait_send()
+
     out[...] = jnp.transpose(base[:, 0 : Q * E], (1, 0)).reshape(Q, E, M)
 
 
@@ -561,6 +637,10 @@
         pltpu.SemaphoreType.DMA((STEPS, 4)),
         pltpu.SemaphoreType.DMA((STEPS, 4)),
         pltpu.SemaphoreType.DMA((2,)),
+        pltpu.VMEM((2, 8, 256), f32),
+        pltpu.VMEM((24, 128), f32),
+        pltpu.SemaphoreType.DMA((3,)),
+        pltpu.SemaphoreType.DMA((3,)),
     ]
     final = pl.pallas_call(
         functools.partial(kernel, axes),

time: 75.2 us -> 67.2 us (0.89)
  the two profiles are of different devices: /device:TPU:15 before, /device:TPU:262 now
where the time goes in v3:
time: 67.2 us; the launch traced here: 67 us
  Pallas kernels  65.4 us (97%)
  local copies, waits for them, and re-layouts  1.58 us (2%)
    pallas_call x1, Pallas kernels, on_device(): pl.pallas_call(functools.partial(kernel, axes), out_shape=jax.ShapeDtypeS...  65.4 us
    unnamed x1, local copies, waits for them, and re-layouts  1.58 us

profile of v3, /device:TPU:262, one launch (start us, length us, event | category | flops | bytes accessed | tf_op | source)
XLA Modules:
  0.0 67.0 jit_solution(10934230115939792576)
XLA Ops:
  0.0 65.4 %lts_update.1 = f32[9,32,56]{2,1,0:T(8,128)} custom-call(f32[9,32,56]{2,1,0:T(8,128)} %bitcast.11, f32[9,9,3,32]{3,2,1,0:T(4,128)} %bitcast.8, f32[3,56,56]{2,1,0:T(8,128)} %refs_2_.1, f32[21,4,56]{2,1,0:T(4,128)} %bitcast.12, f32[9,9,4,32]{3,2,1,0:T(4,128)} %bitcast.9, f32[9,9,4,32]{3,2,1,0:T(4,128)} %bitcast.10, s32[1,32]{1,0:T(1,128)} %bitcast.13, ...), custom_call_target="tpu_custom_call" | custom-call | tf_op jit(solution)/shard_map/lts_update/pallas_call | solution.py:645
  65.4 1.6 %copy.10 = f32[56,9,32]{0,2,1:T(8,128)} copy(f32[56,9,32]{0,2,1:T(8,128)} %bitcast.7) | data formatting | bytes 129024

commit v4 on v3

--- a/solution.py
+++ b/solution.py
@@ -200,9 +200,10 @@
     near = [links[0][0], links[1][0], (dev > 0) & (dev != half)]
     near.append((dev < n_dev - 1) & (dev != half - 1))
     middle = n_group // 2
-    giver = (dev == half - 1) & (group < middle)
-    taker = (dev == half) & (group < middle)
-    relay = (dev == half - 2) & (group >= middle)
+    giver = dev == half - 1
+    taker = dev == half
+    relay = ((dev == half - 2) & (group >= middle)) | ((dev == half + 2) & (group < middle))
+    opposite = lax.rem(group + middle, n_group)
     barrier = pltpu.get_barrier_semaphore()
 
     def greet(there, peer):
@@ -212,10 +213,10 @@
 
     for p, (there, peer, _) in enumerate(links):
         greet(there & jnp.logical_not(taker) if p == 2 else there, peer)
-    above = {"group": group + middle, "dev": half - 2}
+    above = {"group": opposite, "dev": half - 2 + 4 * lax.div(group, middle)}
     greet(giver | taker, above)
-    greet(relay, {"group": group - middle, "dev": half - 1})
-    greet(relay, {"group": group - middle, "dev": half})
+    greet(relay, {"group": opposite, "dev": half - 1})
+    greet(relay, {"group": opposite, "dev": half})
     callers = sum(there.astype(jnp.int32) for there, _, _ in links)
     callers = callers + taker.astype(jnp.int32) + 2 * relay.astype(jnp.int32)
 
@@ -245,18 +246,28 @@
     for i in range(Q):
         tile = jnp.concatenate(last[i] + [jnp.zeros((1, E), f32)], axis=1)
         star[i * 7 + 6] = jnp.broadcast_to(tile, (8, 128))
-    roots = []
-    for i in range(Q):
-        roots.append(jnp.concatenate([root[i, :, f, :] for f in range(4)], axis=1))
-        row = jnp.concatenate([plus_in[i, :, f, :] for f in range(4)], axis=1) * rate4
-        for j in range(Q):
-            plus[i * Q + j] = jnp.broadcast_to(row[j : j + 1], (8, 128))
-    for i in range(Q):
-        for j in range(i, Q):
-            row = jnp.sum(roots[i] * roots[j], axis=0, keepdims=True) * rate4
-            row = jnp.broadcast_to(row, (8, 128))
-            minus[i * Q + j] = row
-            minus[j * Q + i] = row
+    def late_tables():
+        roots = []
+        for i in range(Q):
+            roots.append(jnp.concatenate([root[i, :, f, :] for f in range(4)], axis=1))
+            row = jnp.concatenate([plus_in[i, :, f, :] for f in range(4)], axis=1) * rate4
+            for j in range(Q):
+                plus[i * Q + j] = jnp.broadcast_to(row[j : j + 1], (8, 128))
+        for i in range(Q):
+            for j in range(i, Q):
+                row = jnp.sum(roots[i] * roots[j], axis=0, keepdims=True) * rate4
+                row = jnp.broadcast_to(row, (8, 128))
+                minus[i * Q + j] = row
+                minus[j * Q + i] = row
+        local = lax.broadcasted_iota(jnp.int32, (128, 128), 0) == code
+        local = jnp.where(local, 1.0, 0.0).astype(f32).astype(bf16)
+        pick[...] = jnp.concatenate([local, local], axis=0)
+        pt_stack[...] = stacked(jnp.transpose(p_rows[...], (1, 0)))
+        pending[...] = jnp.zeros_like(pending)
+        for u in range(STEPS):
+            starting = (True, fast, fast | middling, fast)[u]
+            mask[u] = jnp.where(starting, 1.0, 0.0).astype(f32) if u else jnp.ones((8, W), f32)
+
     stiff_rows = [stiff[d] - jnp.transpose(stiff[d], (1, 0)) for d in range(3)]
     stiff_rows = jnp.concatenate(stiff_rows + [jnp.zeros((M, K3 - 3 * M), f32)], axis=1)
     s_stack[...] = stacked(jnp.concatenate([stiff_rows, jnp.zeros((8, K3), f32)], axis=0))
@@ -264,27 +275,20 @@
     for f in range(4):
         p_rows[f * FM : f * FM + 21, 0:M] = proj[:, f, :]
     p_stack[...] = stacked(p_rows[...])
-    pt_stack[...] = stacked(jnp.transpose(p_rows[...], (1, 0)))
+    fast, middling = kind12 == 2, kind12 == 1
     for u in range(STEPS):
-        first = [kind12 == 2, kind12 == 1]
-        starting = (True, first[0], first[0] | first[1], first[0])[u]
-        mask[u] = jnp.ones((8, W), f32) if u == 0 else jnp.where(starting, 1.0, 0.0).astype(f32)
         for k in range(TERMS):
             coef[u * TERMS + k] = jnp.where(
-                first[0],
+                fast,
                 weights(k, 0),
-                jnp.where(first[1], weights(k, u % 2), weights(k, u)),
+                jnp.where(middling, weights(k, u % 2), weights(k, u)),
             ).astype(f32)
     code = jnp.concatenate([codes[0, f : f + 1, :] for f in range(4)], axis=1)
-    local = lax.broadcasted_iota(jnp.int32, (128, 128), 0) == code
-    local = jnp.where(local, 1.0, 0.0).astype(f32).astype(bf16)
-    pick[...] = jnp.concatenate([local, local], axis=0)
     remote = lax.broadcasted_iota(jnp.int32, (32, 128), 0) + 128 == code
     remote = jnp.where(remote, 1.0, 0.0).astype(f32).astype(bf16)
     owed[...] = jnp.concatenate([remote, remote], axis=1)
     base[...] = jnp.zeros_like(base)
     base[:, 0 : Q * E] = jnp.transpose(dofs[...].reshape(Q * E, M), (1, 0))
-    pending[...] = jnp.zeros_like(pending)
 
     def tall(row):
         return jnp.broadcast_to(row[None], (M // 8, 8, W)).reshape(M, W)
@@ -332,7 +336,7 @@
             dst_ref=(recv_buf.at[0, 2], fixed_recv, recv_buf.at[1, 2])[part],
             send_sem=onward_sem.at[part],
             recv_sem=(recv_sem.at[0, 2], fixed_sem.at[1], recv_sem.at[1, 2])[part],
-            device_id={"group": group - middle, "dev": half},
+            device_id={"group": opposite, "dev": half},
             device_id_type=MESH,
         )
 
@@ -342,7 +346,7 @@
             x = operator(x, table, s_stack)
             return x, total + tall(coef[u * TERMS + k]) * x
 
-        return lax.fori_loop(1, TERMS, term, (x, tall(coef[u * TERMS]) * x))[1]
+        return lax.fori_loop(1, TERMS, term, (x, tall(coef[u * TERMS]) * x), unroll=True)[1]
 
     def project(total):
         padded = jnp.concatenate([total, jnp.zeros((8, W), f32)], axis=0)
@@ -477,6 +481,7 @@
 
         @pl.when(h == 0)
         def _():
+            late_tables()
             pack_fixed()
 
         @pl.when(by_relay)
@@ -485,7 +490,7 @@
 
         for p, there in far.items():
 
-            @pl.when(there & (h == 0) & jnp.logical_not(giver))
+            @pl.when(there & (h == 0) & taker)
             def _():
                 fixed(p).start()
 
@@ -530,7 +535,7 @@
             def _():
                 hand_over(2).start()
 
-            @pl.when(h > 0)
+            @pl.when(taker & (h > 0))
             def _():
                 respond(u)
 
@@ -565,6 +570,9 @@
             @pl.when(h == 0)
             def _():
                 unpack_fixed()
+
+            @pl.when(giver | (h == 0))
+            def _():
                 respond(u)
 
             for p, there in far.items():

time: 67.2 us -> 69.3 us (1.031)
  the two profiles are of different devices: /device:TPU:262 before, /device:TPU:102 now
where the time goes in v4:
time: 69.3 us; the launch traced here: 69.1 us
  Pallas kernels  67.5 us (97%)
  local copies, waits for them, and re-layouts  1.58 us (2%)
    pallas_call x1, Pallas kernels, on_device(): pl.pallas_call(functools.partial(kernel, axes), out_shape=jax.ShapeDtypeS...  67.5 us
    unnamed x1, local copies, waits for them, and re-layouts  1.58 us

profile of v4, /device:TPU:102, one launch (start us, length us, event | category | flops | bytes accessed | tf_op | source)
XLA Modules:
  0.0 69.1 jit_solution(3450247747271628827)
XLA Ops:
  0.0 67.5 %lts_update.1 = f32[9,32,56]{2,1,0:T(8,128)} custom-call(f32[9,32,56]{2,1,0:T(8,128)} %bitcast.11, f32[9,9,3,32]{3,2,1,0:T(4,128)} %bitcast.8, f32[3,56,56]{2,1,0:T(8,128)} %refs_2_.1, f32[21,4,56]{2,1,0:T(4,128)} %bitcast.12, f32[9,9,4,32]{3,2,1,0:T(4,128)} %bitcast.9, f32[9,9,4,32]{3,2,1,0:T(4,128)} %bitcast.10, s32[1,32]{1,0:T(1,128)} %bitcast.13, ...), custom_call_target="tpu_custom_call" | custom-call | tf_op jit(solution)/shard_map/lts_update/pallas_call | solution.py:653
  67.6 1.6 %copy.10 = f32[56,9,32]{0,2,1:T(8,128)} copy(f32[56,9,32]{0,2,1:T(8,128)} %bitcast.7) | data formatting | bytes 129024

commit v5 on v4

--- a/solution.py
+++ b/solution.py
@@ -200,9 +200,9 @@
     near = [links[0][0], links[1][0], (dev > 0) & (dev != half)]
     near.append((dev < n_dev - 1) & (dev != half - 1))
     middle = n_group // 2
-    giver = dev == half - 1
-    taker = dev == half
-    relay = ((dev == half - 2) & (group >= middle)) | ((dev == half + 2) & (group < middle))
+    giver = (dev == half - 1) & (group < middle)
+    taker = (dev == half) & (group < middle)
+    relay = (dev == half - 2) & (group >= middle)
     opposite = lax.rem(group + middle, n_group)
     barrier = pltpu.get_barrier_semaphore()
 
@@ -490,7 +490,7 @@
 
         for p, there in far.items():
 
-            @pl.when(there & (h == 0) & taker)
+            @pl.when(there & (h == 0) & jnp.logical_not(giver))
             def _():
                 fixed(p).start()
 
@@ -535,7 +535,7 @@
             def _():
                 hand_over(2).start()
 
-            @pl.when(taker & (h > 0))
+            @pl.when(h > 0)
             def _():
                 respond(u)
 
@@ -571,7 +571,7 @@
             def _():
                 unpack_fixed()
 
-            @pl.when(giver | (h == 0))
+            @pl.when(h == 0)
             def _():
                 respond(u)
 

time: 69.3 us -> 66.7 us (0.962)
  the two profiles are of different devices: /device:TPU:102 before, /device:TPU:262 now
where the time goes in v5:
time: 66.7 us; the launch traced here: 66.5 us
  Pallas kernels  64.9 us (97%)
  local copies, waits for them, and re-layouts  1.58 us (2%)
    pallas_call x1, Pallas kernels, on_device(): pl.pallas_call(functools.partial(kernel, axes), out_shape=jax.ShapeDtypeS...  64.9 us
    unnamed x1, local copies, waits for them, and re-layouts  1.58 us

profile of v5, /device:TPU:262, one launch (start us, length us, event | category | flops | bytes accessed | tf_op | source)
XLA Modules:
  0.0 66.5 jit_solution(15484535808778475317)
XLA Ops:
  0.0 64.9 %lts_update.1 = f32[9,32,56]{2,1,0:T(8,128)} custom-call(f32[9,32,56]{2,1,0:T(8,128)} %bitcast.11, f32[9,9,3,32]{3,2,1,0:T(4,128)} %bitcast.8, f32[3,56,56]{2,1,0:T(8,128)} %refs_2_.1, f32[21,4,56]{2,1,0:T(4,128)} %bitcast.12, f32[9,9,4,32]{3,2,1,0:T(4,128)} %bitcast.9, f32[9,9,4,32]{3,2,1,0:T(4,128)} %bitcast.10, s32[1,32]{1,0:T(1,128)} %bitcast.13, ...), custom_call_target="tpu_custom_call" | custom-call | tf_op jit(solution)/shard_map/lts_update/pallas_call | solution.py:653
  64.9 1.6 %copy.10 = f32[56,9,32]{0,2,1:T(8,128)} copy(f32[56,9,32]{0,2,1:T(8,128)} %bitcast.7) | data formatting | bytes 129024
